TPU v7x, 128 devices: a whole 4x4x4 slice. The times are simulated.
128 devices in a mesh: morton: 64 (over z, x, y), help: 2 (over core).
Axes of the slice: x: 4, y: 4, z: 4, core: 2. Of those that a mesh axis runs over, the one named last changes fastest.
Arguments:
- multipoles: bfloat16 [131072, 296], P(('morton', 'help')), may hold values from -6 to 6
- sources: int32 [131072, 16], P(('morton', 'help')), may hold values from 0 to 6143, as said below
- labels: int32 [131072, 16], P(('morton', 'help')), may hold values from 0 to 16, as said below
- operators: bfloat16 [16, 296, 296], replicated, may hold values from -0.375 to 0.375
Outputs:
- locals_out: float32 [131072, 296], P(('morton', 'help'))
Inputs may be any that keep to these rules, and one draw needn't show every extreme that they name: The octant named by a slot, (t // (2 * 1024) - 1) * 2 * 1024 + sources[t, j], lies between 0 and 131071. `labels`: no target names one operator in two slots; the value 16 marks an empty slot.
All inputs are finite; a program needn't handle non-finite values.
Results may differ from a plain program's by a relative error of at most 0.0003.
Values may be sent and summed in bfloat16 or wider, within the bound.
A program may use at most 64 MiB of HBM per device.

v0:
```python
import jax
import jax.numpy as jnp
from jax import lax
from jax.sharding import PartitionSpec as P

P_SIZE = 296
OPS = 16
SLOTS = 16


def from_behind(value, axis, steps):
    count = lax.axis_size(axis)
    first, last = (max(0, -steps), min(count, count - steps))
    return lax.ppermute(value, axis, [(source, source + steps) for source in range(first, last)])


def translate(window, local_index, labels, operators):
    total_rows = local_index.shape[0]
    window_rows = window.shape[0]
    block_rows = min(512, total_rows)
    block_count = total_rows // block_rows
    stacked = operators.reshape(OPS * P_SIZE, P_SIZE)
    choices_range = jnp.arange(OPS, dtype=jnp.int32)

    def one_block(pieces):
        indices, kinds = pieces
        matched = kinds[:, :, None] == choices_range[None, None, :]
        present = jnp.any(matched, axis=1)
        slot_rows = jnp.sum(jnp.where(matched, indices[:, :, None], 0), axis=1)
        wanted = jnp.where(present, slot_rows, window_rows)
        gathered = jnp.take(
            window, wanted.reshape(block_rows * OPS), axis=0, mode="fill", fill_value=0
        )
        return jnp.dot(
            gathered.reshape(block_rows, OPS * P_SIZE), stacked, preferred_element_type=jnp.float32
        )

    result = lax.map(
        one_block,
        (
            local_index.reshape(block_count, block_rows, SLOTS),
            labels.reshape(block_count, block_rows, SLOTS),
        ),
    )
    return result.reshape(total_rows, P_SIZE)


def per_device(multipoles, sources, labels, operators):
    paired = lax.all_gather(multipoles, "help", axis=0, tiled=True)
    lower_parts = [from_behind(paired, "morton", 1)]
    upper_parts = [from_behind(paired, "morton", -1)]
    window = jnp.concatenate(lower_parts[::-1] + [paired] + upper_parts, axis=0)
    return translate(window, sources, labels, operators)


def solution(mesh):
    placed = (
        P(("morton", "help"), None),
        P(("morton", "help"), None),
        P(("morton", "help"), None),
        P(),
    )
    return jax.shard_map(
        per_device,
        mesh=mesh,
        in_specs=placed,
        out_specs=P(("morton", "help"), None),
        check_vma=False,
    )
```

profile of v0, /device:TPU:30, one launch (start us, length us, event | category | flops | bytes accessed | tf_op | source)
XLA Modules:
  0.0 217.7 jit_solution(5965663476264428362)
XLA Ops:
  6.5 0.7 all-gather.2.cloned.1.call-update
  7.3 15.9 %all-gather.2.cloned.1.call-done = bf16[2048,296]{0,1:T(8,128)(2,1)} async-done(((bf16[1024,296]{0,1:T(8,128)(2,1)}), bf16[2048,296]{0,1:T(8,128)(2,1)}) %all-gather.2.cloned.1.call-update) | async-done | bytes 1212432 | tf_op jit(solution)/shard_map/all_gather | solution.py:49
  23.1 3.4 %collective-permute-start = (bf16[2048,296]{0,1:T(8,128)(2,1)}, bf16[2048,296]{0,1:T(8,128)(2,1)S(1)}, u32[]{:S(2)}, u32[]{:S(2)}) collective-permute-start(bf16[2048,296]{0,1:T(8,128)(2,1)} %all-gather.2.cloned.1.call-done), channel_id=1, source_target_pairs={{0,2},{2,4},{4,6},{6,8},{8,10},{10,12},{12,14},{14,16},{16,18},{18... | collective-permute-start | bytes 3637256 | tf_op jit(solution)/shard_map/ppermute | solution.py:14
  26.5 2.5 %collective-permute-start.1 = (bf16[2048,296]{0,1:T(8,128)(2,1)}, bf16[2048,296]{0,1:T(8,128)(2,1)S(1)}, u32[]{:S(2)}, u32[]{:S(2)}) collective-permute-start(bf16[2048,296]{0,1:T(8,128)(2,1)} %all-gather.2.cloned.1.call-done), channel_id=1, source_target_pairs={{2,0},{4,2},{6,4},{8,6},{10,8},{12,10},{14,12},{16,14},{18,16},{20... | collective-permute-start | bytes 3637256 | tf_op jit(solution)/shard_map/ppermute | solution.py:14
  29.0 0.9 reshape.60
  29.9 0.9 reshape.61
  30.8 23.3 %collective-permute-done = bf16[2048,296]{0,1:T(8,128)(2,1)S(1)} collective-permute-done((bf16[2048,296]{0,1:T(8,128)(2,1)}, bf16[2048,296]{0,1:T(8,128)(2,1)S(1)}, u32[]{:S(2)}, u32[]{:S(2)}) %collective-permute-start) | collective-permute-done | bytes 1212448 | tf_op jit(solution)/shard_map/ppermute | solution.py:14
  54.1 7.3 %collective-permute-done.1 = bf16[2048,296]{0,1:T(8,128)(2,1)S(1)} collective-permute-done((bf16[2048,296]{0,1:T(8,128)(2,1)}, bf16[2048,296]{0,1:T(8,128)(2,1)S(1)}, u32[]{:S(2)}, u32[]{:S(2)}) %collective-permute-start.1) | collective-permute-done | bytes 1212448 | tf_op jit(solution)/shard_map/ppermute | solution.py:14
  61.4 3.1 %pad_maximum_fusion = bf16[6144,296]{0,1:T(8,128)(2,1)} fusion(bf16[2048,296]{0,1:T(8,128)(2,1)S(1)} %collective-permute-done.1, bf16[2048,296]{0,1:T(8,128)(2,1)} %all-gather.2.cloned.1.call-done, bf16[2048,296]{0,1:T(8,128)(2,1)S(1)} %collective-permute-done), kind=kLoop, calls=%fused_computation.17 | loop fusion | flops 10911744 | bytes 7274496 | tf_op jit(solution)/shard_map/concatenate | solution.py:52
  64.5 6.5 %copy.27 = bf16[6144,296]{1,0:T(8,128)(2,1)} copy(bf16[6144,296]{0,1:T(8,128)(2,1)} %pad_maximum_fusion) | data formatting | bytes 7274496
  71.0 138.6 %while.11 = (s32[]{:T(128)}, f32[2,512,296]{1,0,2:T(2,128)S(1)}, s32[2,512,16]{1,0,2:T(2,128)S(1)}, s32[2,512,16]{1,0,2:T(2,128)S(1)}, bf16[6144,296]{1,0:T(8,12...) while((s32[]{:T(128)}, f32[2,512,296]{1,0,2:T(2,128)S(1)}, ...), condition=%wide.region_3.4_spmd.clone, body=%wide.region_0.3_spmd.clone.sunk | while | flops 1438654464 | bytes 61483128 | solution.py:38
  71.6 35.5 %gather_fusion = bf16[8192,296]{1,0:T(8,128)(2,1)} fusion(bf16[6144,296]{1,0:T(8,128)(2,1)} %get-tuple-element.156, s32[8192]{0:T(1024)S(1)} %broadcast_clamp_fusion.2), kind=kCustom, calls=%fused_computation.clone.clone.1 | custom fusion | bytes 9732096 | tf_op jit(solution)/shard_map/while/body/eval_jaxpr/jit(_take)/gather | solution.py:31
  107.1 10.4 %gather.13 = bf16[512,4736]{1,0:T(8,128)(2,1)} reshape(bf16[8192,296]{1,0:T(8,128)(2,1)} %gather_fusion) | data formatting | bytes 9699328 | tf_op jit(solution)/shard_map/while/body/eval_jaxpr/jit(_take)/gather | solution.py:31
  117.5 7.4 %copy.46 = bf16[512,4736]{0,1:T(8,128)(2,1)} copy(bf16[512,4736]{1,0:T(8,128)(2,1)} %gather.13) | data formatting | bytes 9699328 | tf_op jit(solution)/shard_map/while/body/eval_jaxpr/jit(_take)/gather | solution.py:31
  124.9 2.9 %bitcast_select_fusion.2 = bf16[512,4736]{0,1:T(8,128)(2,1)S(1)} fusion(bf16[512,4736]{0,1:T(8,128)(2,1)} %copy.46, pred[512,16]{0,1:T(8,128)(4,1)S(1)} %get-tuple-element.135), kind=kLoop, calls=%fused_computation.2.clone.1 | loop fusion | flops 2424832 | bytes 9707520 | tf_op jit(solution)/shard_map/while/body/eval_jaxpr/jit(_take)/select_n | solution.py:31
  128.3 1.7 convolution_bitcast_fusion.2
  130.7 9.5 %dynamic_update_slice.6 = f32[2,512,296]{1,0,2:T(2,128)S(1)} dynamic-update-slice(f32[2,512,296]{1,0,2:T(2,128)S(1)} %get-tuple-element.145, f32[1,512,296]{1,0,2:T(1,128)S(1)} %copy.47, s32[]{:T(128)} %get-tuple-element.144, s32[]{:T(128)} %constant.31.clone.1..sunk, s32[]{:T(128)} %constant.31.clone.1..sunk) | dynamic-update-slice | bytes 1212420 | tf_op jit(solution)/shard_map/while/body/jit(dynamic_update_index_in_dim)/dynamic_update_slice | solution.py:38
  140.9 35.5 %gather_fusion = bf16[8192,296]{1,0:T(8,128)(2,1)} fusion(bf16[6144,296]{1,0:T(8,128)(2,1)} %get-tuple-element.156, s32[8192]{0:T(1024)S(1)} %broadcast_clamp_fusion.2), kind=kCustom, calls=%fused_computation.clone.clone.1 | custom fusion | bytes 9732096 | tf_op jit(solution)/shard_map/while/body/eval_jaxpr/jit(_take)/gather | solution.py:31
  176.4 10.4 %gather.13 = bf16[512,4736]{1,0:T(8,128)(2,1)} reshape(bf16[8192,296]{1,0:T(8,128)(2,1)} %gather_fusion) | data formatting | bytes 9699328 | tf_op jit(solution)/shard_map/while/body/eval_jaxpr/jit(_take)/gather | solution.py:31
  186.8 7.4 %copy.46 = bf16[512,4736]{0,1:T(8,128)(2,1)} copy(bf16[512,4736]{1,0:T(8,128)(2,1)} %gather.13) | data formatting | bytes 9699328 | tf_op jit(solution)/shard_map/while/body/eval_jaxpr/jit(_take)/gather | solution.py:31
  194.2 2.9 %bitcast_select_fusion.2 = bf16[512,4736]{0,1:T(8,128)(2,1)S(1)} fusion(bf16[512,4736]{0,1:T(8,128)(2,1)} %copy.46, pred[512,16]{0,1:T(8,128)(4,1)S(1)} %get-tuple-element.135), kind=kLoop, calls=%fused_computation.2.clone.1 | loop fusion | flops 2424832 | bytes 9707520 | tf_op jit(solution)/shard_map/while/body/eval_jaxpr/jit(_take)/select_n | solution.py:31
  197.7 1.7 convolution_bitcast_fusion.2
  200.0 9.5 %dynamic_update_slice.6 = f32[2,512,296]{1,0,2:T(2,128)S(1)} dynamic-update-slice(f32[2,512,296]{1,0,2:T(2,128)S(1)} %get-tuple-element.145, f32[1,512,296]{1,0,2:T(1,128)S(1)} %copy.47, s32[]{:T(128)} %get-tuple-element.144, s32[]{:T(128)} %constant.31.clone.1..sunk, s32[]{:T(128)} %constant.31.clone.1..sunk) | dynamic-update-slice | bytes 1212420 | tf_op jit(solution)/shard_map/while/body/jit(dynamic_update_index_in_dim)/dynamic_update_slice | solution.py:38
  209.6 1.3 copy.33
  (30 shorter events, 3.6 us)
Async XLA Ops:
  6.5 16.6 %all-gather.2.cloned.1.call-start = ((), (), s32[]{:S(2)}) async-start(), calls=%async_computation | async-start | bytes 1818624 | tf_op jit(solution)/shard_map/all_gather | solution.py:49
  23.1 31.0 %collective-permute-start = (bf16[2048,296]{0,1:T(8,128)(2,1)}, bf16[2048,296]{0,1:T(8,128)(2,1)S(1)}, u32[]{:S(2)}, u32[]{:S(2)}) collective-permute-start(bf16[2048,296]{0,1:T(8,128)(2,1)} %all-gather.2.cloned.1.call-done), channel_id=1, source_target_pairs={{0,2},{2,4},{4,6},{6,8},{8,10},{10,12},{12,14},{14,16},{16,18},{18... | collective-permute-start | bytes 3637256 | tf_op jit(solution)/shard_map/ppermute | solution.py:14
  26.5 34.9 %collective-permute-start.1 = (bf16[2048,296]{0,1:T(8,128)(2,1)}, bf16[2048,296]{0,1:T(8,128)(2,1)S(1)}, u32[]{:S(2)}, u32[]{:S(2)}) collective-permute-start(bf16[2048,296]{0,1:T(8,128)(2,1)} %all-gather.2.cloned.1.call-done), channel_id=1, source_target_pairs={{2,0},{4,2},{6,4},{8,6},{10,8},{12,10},{14,12},{16,14},{18,16},{20... | collective-permute-start | bytes 3637256 | tf_op jit(solution)/shard_map/ppermute | solution.py:14
  64.5 6.5 %copy-start = (f32[2,512,296]{1,0,2:T(2,128)S(1)}, f32[2,512,296]{1,0,2:T(2,128)}, u32[]{:S(2)}) copy-start(f32[2,512,296]{1,0,2:T(2,128)} %custom-call.2) | copy-start | bytes 3637252
  124.9 3.5 %copy-start.1 = (bf16[4736,296]{1,0:T(8,128)(2,1)S(1)}, bf16[4736,296]{1,0:T(8,128)(2,1)}, u32[]{:S(2)}) copy-start(bf16[4736,296]{1,0:T(8,128)(2,1)} %get-tuple-element.157) | copy-start | bytes 8411140 | tf_op jit(solution)/shard_map/while
  194.2 3.5 %copy-start.1 = (bf16[4736,296]{1,0:T(8,128)(2,1)S(1)}, bf16[4736,296]{1,0:T(8,128)(2,1)}, u32[]{:S(2)}) copy-start(bf16[4736,296]{1,0:T(8,128)(2,1)} %get-tuple-element.157) | copy-start | bytes 8411140 | tf_op jit(solution)/shard_map/while
Sparse Core Ops, SparseCore 0:
  9.0 14.0 all-gather.1
where the time goes:
time: 219 us; the launch traced here: 218 us
  local copies, waits for them, and re-layouts  138 us (63%)
  waiting for transfers between devices  47.2 us (22%)
  between operations  13.4 us (6%)
  other arithmetic  9.21 us (4%)
  starting transfers between devices  5.83 us (3%)
  matrix products  3.45 us (2%)
    gather x6, local copies, waits for them, and re-layouts, one_block(): jnp.take(window, wanted.reshape(block_rows * OPS), axis=0, mode='fill', f...  107 us
    ppermute x2, waiting for transfers between devices, from_behind(): lax.ppermute(value, axis, [(source, source + steps) for source in range(f...  30.6 us
    dynamic_update_slice x4, local copies, waits for them, and re-layouts, translate(): lax.map(one_block, (local_index.reshape(block_count, block_rows, SLOTS),...  20.3 us
    all_gather x1, waiting for transfers between devices, per_device(): paired = lax.all_gather(multipoles, 'help', axis=0, tiled=True)  15.9 us
    unnamed x4, local copies, waits for them, and re-layouts  7.72 us
    ppermute x2, starting transfers between devices, from_behind(): lax.ppermute(value, axis, [(source, source + steps) for source in range(f...  5.83 us
    select_n x4, other arithmetic, one_block(): jnp.take(window, wanted.reshape(block_rows * OPS), axis=0, mode='fill', f...  5.81 us
  transfers between devices with their start and end apart: 3, of which 3 were waited for; matrix products, arithmetic and copies ran while one was open for 1% of the time, Pallas kernels for 0%

commit v1 on v0

v1 whole, which is shorter than its diff:
```python
import jax
import jax.numpy as jnp
from jax import lax
from jax.experimental import pallas as pl
from jax.experimental.pallas import tpu as pltpu
from jax.sharding import PartitionSpec as P

P_SIZE = 296
OPS = 16
SLOTS = 16
ROWS = 1024
LANES = 128
CHUNKS = 3
PITCH = 4
PADDED = CHUNKS * LANES
WINDOW = 6 * ROWS
EMPTY = WINDOW
GROUP = 4
TILE = 256
MESH = pl.DeviceIdType.MESH
CUTS = ((0, 128), (128, 128), (256, 40))


def translate_kernel(
    mult_ref, src_ref, lab_ref, op_ref, out_ref,
    recv, win, opraw, opt, left_g, right_g, idxv, idxs,
    own_sem, op_sem, idx_sem, send_sem, recv_sem,
):
    g = lax.axis_index("morton")
    h = lax.axis_index("help")
    count = lax.axis_size("morton")
    above = (lax.rem(g + 1, count), h)
    below = (lax.rem(g + count - 1, count), h)
    sibling = (g, 1 - h)

    barrier = pltpu.get_barrier_semaphore()
    for device in (sibling, above, below):
        pl.semaphore_signal(barrier, inc=1, device_id=device, device_id_type=MESH)
    pl.semaphore_wait(barrier, 3)

    def send(kind, cut, slot, device, source):
        start, size = CUTS[cut]
        return pltpu.make_async_remote_copy(
            src_ref=source.at[pl.ds(start, size)],
            dst_ref=recv.at[slot, pl.ds(start, size)],
            send_sem=send_sem.at[kind, cut],
            recv_sem=recv_sem.at[kind, cut],
            device_id=device,
            device_id_type=MESH,
        )

    ups = [send(0, c, h, above, mult_ref) for c in range(CHUNKS)]
    downs = [send(1, c, 4 + h, below, mult_ref) for c in range(CHUNKS)]
    sides = [send(2, c, 2 + h, sibling, mult_ref) for c in range(CHUNKS)]
    lows = [send(3, c, h, sibling, recv.at[h]) for c in range(CHUNKS)]
    highs = [send(4, c, 4 + h, sibling, recv.at[4 + h]) for c in range(CHUNKS)]
    for c in range(CHUNKS):
        ups[c].start()
        downs[c].start()
    for c in range(CHUNKS):
        sides[c].start()
    own = pltpu.make_async_copy(mult_ref, recv.at[2 + h, pl.ds(0, P_SIZE)], own_sem)
    own.start()
    ops_copy = pltpu.make_async_copy(op_ref, opraw, op_sem)
    ops_copy.start()

    kinds = lax.broadcasted_iota(jnp.int32, (OPS, ROWS), 0)
    picked = jnp.full((OPS, ROWS), EMPTY * PITCH, jnp.int32)
    for j in range(SLOTS):
        hit = lab_ref[j : j + 1, :] == kinds
        picked = jnp.where(hit, src_ref[j : j + 1, :] * PITCH, picked)
    for a in range(2):
        for b in range(8):
            row = (a * 8 + b) * 8
            idxv[row : row + 8, :] = picked[8 * a : 8 * a + 8, LANES * b : LANES * b + LANES]
    idx_copy = pltpu.make_async_copy(idxv, idxs, idx_sem)
    idx_copy.start()

    win[pl.ds(WINDOW * PITCH, 8 * PITCH), :] = jnp.zeros((8 * PITCH, LANES), jnp.float32)
    pad = jnp.zeros((PADDED - P_SIZE, ROWS), jnp.bfloat16)
    for s in range(6):
        recv[s, P_SIZE:, :] = pad

    def eye(n):
        return (
            lax.broadcasted_iota(jnp.int32, (n, n), 0) == lax.broadcasted_iota(jnp.int32, (n, n), 1)
        ).astype(jnp.bfloat16)

    unit = eye(TILE)

    def place(slot, c):
        @pl.loop(0, ROWS // TILE)
        def _(b):
            first = pl.multiple_of(b * TILE, TILE)
            piece = recv[slot, pl.ds(c * LANES, LANES), pl.ds(first, TILE)]
            turned = lax.dot_general(
                unit, piece, (((1,), (1,)), ((), ())), preferred_element_type=jnp.float32
            )
            base = pl.multiple_of((slot * ROWS + first) * PITCH, TILE * PITCH)
            win[pl.ds(base + c, TILE, stride=PITCH), :] = turned

    own.wait()
    for c in range(CHUNKS):
        place(2 + h, c)

    ops_copy.wait()
    unit_op = eye(P_SIZE)
    tail = jnp.zeros((P_SIZE, PADDED - P_SIZE), jnp.bfloat16)

    @pl.loop(0, OPS)
    def _(k):
        turned = lax.dot_general(
            unit_op, opraw[k], (((1,), (1,)), ((), ())), preferred_element_type=jnp.float32
        ).astype(jnp.bfloat16)
        opt[:, pl.ds(pl.multiple_of(k * PADDED, PADDED), PADDED)] = jnp.concatenate([turned, tail], axis=1)

    for c in range(CHUNKS):
        sides[c].wait_recv()
        place(3 - h, c)
    for c in range(CHUNKS):
        ups[c].wait_recv()
        lows[c].start()
        downs[c].wait_recv()
        highs[c].start()
        place(h, c)
        place(4 + h, c)
        if c:
            lows[c - 1].wait_recv()
            place(1 - h, c - 1)
            highs[c - 1].wait_recv()
            place(5 - h, c - 1)
    lows[CHUNKS - 1].wait_recv()
    place(1 - h, CHUNKS - 1)
    highs[CHUNKS - 1].wait_recv()
    place(5 - h, CHUNKS - 1)
    idx_copy.wait()

    groups = OPS // GROUP
    halves = TILE // LANES
    steps = groups * (ROWS // TILE)
    span = LANES - (8 * (halves - 1) + GROUP - 1)

    def gather(step, into):
        n, k = step // groups, lax.rem(step, groups) * GROUP
        base = ((k // 8) * 8 + n * halves) * 8 + lax.rem(k, 8)
        for kk in range(GROUP):
            for half in range(halves):
                column = idxs.at[pl.ds(8 * half + kk, span)]
                for lane in range(LANES):
                    row = column.at[:, pl.ds(lane, 1)][base, 0]
                    to = (kk * TILE + half * LANES + lane) * PITCH
                    into[pl.ds(to, PITCH), :] = win[pl.ds(row, PITCH), :]

    def multiply(step, held):
        n, k = step // groups, lax.rem(step, groups)
        parts = []
        for kk in range(GROUP):
            for c in range(CHUNKS):
                parts.append(
                    held[pl.ds(kk * TILE * PITCH + c, TILE, stride=PITCH), :].astype(jnp.bfloat16)
                )
        depth = GROUP * PADDED
        result = lax.dot_general(
            opt[:, pl.ds(pl.multiple_of(k * depth, depth), depth)],
            jnp.concatenate(parts, axis=1),
            (((1,), (1,)), ((), ())),
            preferred_element_type=jnp.float32,
        )
        where = pl.ds(pl.multiple_of(n * TILE, TILE), TILE)
        out_ref[:, where] += result

    out_ref[...] = jnp.zeros_like(out_ref)
    gather(0, left_g)

    @pl.loop(0, steps // 2)
    def _(pair):
        step = pair * 2
        gather(step + 1, right_g)
        multiply(step, left_g)
        gather(lax.rem(step + 2, steps), left_g)
        multiply(step + 1, right_g)

    for c in range(CHUNKS):
        for copy in (ups[c], downs[c], sides[c], lows[c], highs[c]):
            copy.wait_send()


def per_device(multipoles, sources, labels, operators):
    vmem = pl.BlockSpec(memory_space=pltpu.VMEM)
    anywhere = pl.BlockSpec(memory_space=pl.ANY)
    out = pl.pallas_call(
        translate_kernel,
        out_shape=jax.ShapeDtypeStruct((P_SIZE, ROWS), jnp.float32),
        in_specs=[anywhere, vmem, vmem, anywhere],
        out_specs=vmem,
        scratch_shapes=[
            pltpu.VMEM((6, PADDED, ROWS), jnp.bfloat16),
            pltpu.VMEM(((WINDOW + 8) * PITCH, LANES), jnp.float32),
            pltpu.VMEM((OPS, P_SIZE, P_SIZE), jnp.bfloat16),
            pltpu.VMEM((P_SIZE, OPS * PADDED), jnp.bfloat16),
            pltpu.VMEM((GROUP * TILE * PITCH, LANES), jnp.float32),
            pltpu.VMEM((GROUP * TILE * PITCH, LANES), jnp.float32),
            pltpu.VMEM((LANES, LANES), jnp.int32),
            pltpu.SMEM((LANES, LANES), jnp.int32),
            pltpu.SemaphoreType.DMA,
            pltpu.SemaphoreType.DMA,
            pltpu.SemaphoreType.DMA,
            pltpu.SemaphoreType.DMA((5, CHUNKS)),
            pltpu.SemaphoreType.DMA((5, CHUNKS)),
        ],
        compiler_params=pltpu.CompilerParams(
            collective_id=0, has_side_effects=True, vmem_limit_bytes=56 * 1024 * 1024
        ),
        name="translate",
    )(multipoles.T, sources.T, labels.T, operators)
    return out.T


def solution(mesh):
    placed = (
        P(("morton", "help"), None),
        P(("morton", "help"), None),
        P(("morton", "help"), None),
        P(),
    )
    return jax.shard_map(
        per_device,
        mesh=mesh,
        in_specs=placed,
        out_specs=P(("morton", "help"), None),
        check_vma=False,
    )
```

time: 219 us -> 48.7 us (0.22)
  the two profiles are of different devices: /device:TPU:30 before, /device:TPU:0 now
where the time goes in v1:
time: 48.7 us; the launch traced here: 48.6 us
  Pallas kernels  46.1 us (95%)
  local copies, waits for them, and re-layouts  2.44 us (5%)
    pallas_call x1, Pallas kernels, per_device(): pl.pallas_call(translate_kernel, out_shape=jax.ShapeDtypeStruct((P_SIZE,...  46.1 us
    unnamed x1, local copies, waits for them, and re-layouts  2.44 us

profile of v1, /device:TPU:0, one launch (start us, length us, event | category | flops | bytes accessed | tf_op | source)
XLA Modules:
  0.0 48.6 jit_solution(6022555279551504711)
XLA Ops:
  0.0 46.1 %translate.1 = f32[296,1024]{1,0:T(8,128)} custom-call(bf16[296,1024]{1,0:T(8,128)(2,1)} %bitcast.5, s32[16,1024]{1,0:T(8,128)} %bitcast.6, s32[16,1024]{1,0:T(8,128)} %bitcast.7, bf16[16,296,296]{2,1,0:T(8,128)(2,1)} %op_ref.1), custom_call_target="tpu_custom_call" | custom-call | tf_op jit(solution)/shard_map/translate/pallas_call | solution.py:191
  46.1 2.4 %copy.6 = f32[1024,296]{0,1:T(8,128)} copy(f32[1024,296]{0,1:T(8,128)} %bitcast.4) | data formatting | bytes 2424832

commit v2 on v1

v2 whole, which is shorter than its diff:
```python
import jax
import jax.numpy as jnp
from jax import lax
from jax.experimental import pallas as pl
from jax.experimental.pallas import tpu as pltpu
from jax.sharding import PartitionSpec as P

P_SIZE = 296
OPS = 16
SLOTS = 16
ROWS = 1024
LANES = 128
CHUNKS = 3
PITCH = 4
PADDED = CHUNKS * LANES
PIECES = 4
WINDOW = 6 * ROWS
EMPTY = WINDOW
GROUP = 4
TILE = 256
MESH = pl.DeviceIdType.MESH


def translate_kernel(
    mult_ref, src_hbm, lab_hbm, op_ref, out_ref,
    recv, win, opraw, opt, left_g, right_g, src_ref, lab_ref, idxv, idxs, total,
    own_sem, src_sem, lab_sem, op_sem, idx_sem, out_sem, send_sem, recv_sem,
):
    g = lax.axis_index("morton")
    h = lax.axis_index("help")
    count = lax.axis_size("morton")
    above = (lax.rem(g + 1, count), h)
    below = (lax.rem(g + count - 1, count), h)
    sibling = (g, 1 - h)
    has_above = g < count - 1
    has_below = g > 0

    barrier = pltpu.get_barrier_semaphore()
    pl.semaphore_signal(barrier, inc=1, device_id=sibling, device_id_type=MESH)

    @pl.when(has_above)
    def _():
        pl.semaphore_signal(barrier, inc=1, device_id=above, device_id_type=MESH)

    @pl.when(has_below)
    def _():
        pl.semaphore_signal(barrier, inc=1, device_id=below, device_id_type=MESH)

    pl.semaphore_wait(barrier, 1 + has_above.astype(jnp.int32) + has_below.astype(jnp.int32))

    def lanes(b):
        return pl.ds(b * TILE, TILE)

    def send(kind, b, slot, device, source):
        return pltpu.make_async_remote_copy(
            src_ref=source.at[:, lanes(b)],
            dst_ref=recv.at[slot, pl.ds(0, P_SIZE), lanes(b)],
            send_sem=send_sem.at[kind, b],
            recv_sem=recv_sem.at[kind, b],
            device_id=device,
            device_id_type=MESH,
        )

    order = range(PIECES)
    ups = [send(0, b, h, above, mult_ref) for b in order]
    downs = [send(1, b, 4 + h, below, mult_ref) for b in order]
    sides = [send(2, b, 2 + h, sibling, mult_ref) for b in order]
    lows = [send(3, b, h, sibling, recv.at[h, pl.ds(0, P_SIZE)]) for b in order]
    highs = [send(4, b, 4 + h, sibling, recv.at[4 + h, pl.ds(0, P_SIZE)]) for b in order]
    for b in order:

        @pl.when(has_above)
        def _(b=b):
            ups[b].start()

        @pl.when(has_below)
        def _(b=b):
            downs[b].start()

    for b in order:
        sides[b].start()
    src_copy = pltpu.make_async_copy(src_hbm, src_ref, src_sem)
    lab_copy = pltpu.make_async_copy(lab_hbm, lab_ref, lab_sem)
    own = pltpu.make_async_copy(mult_ref, recv.at[2 + h, pl.ds(0, P_SIZE)], own_sem)
    ops_copy = pltpu.make_async_copy(op_ref, opraw, op_sem)
    src_copy.start()
    lab_copy.start()
    own.start()
    ops_copy.start()

    win[pl.ds(WINDOW * PITCH, 8 * PITCH), :] = jnp.zeros((8 * PITCH, LANES), jnp.float32)
    pad = jnp.zeros((PADDED - P_SIZE, ROWS), jnp.bfloat16)
    for s in range(6):
        recv[s, P_SIZE:, :] = pad

    src_copy.wait()
    lab_copy.wait()
    kinds = lax.broadcasted_iota(jnp.int32, (OPS, ROWS), 0)
    picked = jnp.full((OPS, ROWS), EMPTY * PITCH, jnp.int32)
    for j in range(SLOTS):
        hit = lab_ref[j : j + 1, :] == kinds
        picked = jnp.where(hit, src_ref[j : j + 1, :] * PITCH, picked)
    for a in range(2):
        for b in range(8):
            row = (a * 8 + b) * 8
            idxv[row : row + 8, :] = picked[8 * a : 8 * a + 8, LANES * b : LANES * b + LANES]
    idx_copy = pltpu.make_async_copy(idxv, idxs, idx_sem)
    idx_copy.start()

    def eye(n):
        return (
            lax.broadcasted_iota(jnp.int32, (n, n), 0) == lax.broadcasted_iota(jnp.int32, (n, n), 1)
        ).astype(jnp.bfloat16)

    unit = eye(TILE)

    def place(pairs):
        for slot, b in pairs:
            turned = lax.dot_general(
                unit, recv[slot, :, lanes(b)], (((1,), (1,)), ((), ())), preferred_element_type=jnp.float32
            )
            base = pl.multiple_of((slot * ROWS + b * TILE) * PITCH, TILE * PITCH)
            for c in range(CHUNKS):
                win[pl.ds(base + c, TILE, stride=PITCH), :] = turned[:, c * LANES : c * LANES + LANES]

    ops_copy.wait()
    unit_op = eye(P_SIZE)
    tail = jnp.zeros((P_SIZE, PADDED - P_SIZE), jnp.bfloat16)

    @pl.loop(0, OPS)
    def _(k):
        turned = lax.dot_general(
            unit_op, opraw[k], (((1,), (1,)), ((), ())), preferred_element_type=jnp.float32
        ).astype(jnp.bfloat16)
        opt[:, pl.ds(pl.multiple_of(k * PADDED, PADDED), PADDED)] = jnp.concatenate([turned, tail], axis=1)

    own.wait()
    place([(2 + h, b) for b in order])
    for b in order:
        sides[b].wait_recv()
    place([(3 - h, b) for b in order])

    def receive(b):
        @pl.when(has_below)
        def _():
            ups[b].wait_recv()
            lows[b].start()

        @pl.when(has_above)
        def _():
            downs[b].wait_recv()
            highs[b].start()

    def receive_from_sibling(b):
        @pl.when(has_below)
        def _():
            lows[b].wait_recv()

        @pl.when(has_above)
        def _():
            highs[b].wait_recv()

    for b in order:
        receive(b)
        if b:
            receive_from_sibling(b - 1)
            place([(h, b), (4 + h, b), (1 - h, b - 1), (5 - h, b - 1)])
        else:
            place([(h, b), (4 + h, b)])
    receive_from_sibling(PIECES - 1)
    place([(1 - h, PIECES - 1), (5 - h, PIECES - 1)])
    idx_copy.wait()

    groups = OPS // GROUP
    blocks = ROWS // TILE
    halves = TILE // LANES
    span = LANES - (8 * (halves - 1) + GROUP - 1)
    depth = GROUP * PADDED

    def gather(n, k, into):
        base = ((k * GROUP // 8) * 8 + n * halves) * 8 + k * GROUP % 8
        for kk in range(GROUP):
            for half in range(halves):
                column = idxs.at[pl.ds(8 * half + kk, span)]
                for lane in range(LANES):
                    row = column.at[:, pl.ds(lane, 1)][base, 0]
                    to = (kk * TILE + half * LANES + lane) * PITCH
                    into[pl.ds(to, PITCH), :] = win[pl.ds(row, PITCH), :]

    def multiply(n, k, held):
        parts = []
        for kk in range(GROUP):
            for c in range(CHUNKS):
                parts.append(
                    held[pl.ds(kk * TILE * PITCH + c, TILE, stride=PITCH), :].astype(jnp.bfloat16)
                )
        result = lax.dot_general(
            opt[:, k * depth : (k + 1) * depth],
            jnp.concatenate(parts, axis=1),
            (((1,), (1,)), ((), ())),
            preferred_element_type=jnp.float32,
        )
        where = pl.ds(pl.multiple_of(n * TILE, TILE), TILE)
        if k:
            total[:, where] += result
        else:
            total[:, where] = result

    def leave(n):
        where = pl.ds(pl.multiple_of(n * TILE, TILE), TILE)
        return pltpu.make_async_copy(total.at[:, where], out_ref.at[:, where], out_sem.at[n])

    gather(0, 0, left_g)

    @pl.loop(0, blocks)
    def _(n):
        for k in range(groups):
            held, into = (right_g, left_g) if k % 2 else (left_g, right_g)
            if k < groups - 1:
                gather(n, k + 1, into)
            else:
                gather(lax.rem(n + 1, blocks), 0, into)
            multiply(n, k, held)
        leave(n).start()

    for n in range(blocks):
        leave(n).wait()
    for b in order:
        sides[b].wait_send()

        @pl.when(has_above)
        def _(b=b):
            ups[b].wait_send()
            highs[b].wait_send()

        @pl.when(has_below)
        def _(b=b):
            downs[b].wait_send()
            lows[b].wait_send()


def per_device(multipoles, sources, labels, operators):
    anywhere = pl.BlockSpec(memory_space=pl.ANY)
    out = pl.pallas_call(
        translate_kernel,
        out_shape=jax.ShapeDtypeStruct((P_SIZE, ROWS), jnp.float32),
        in_specs=[anywhere] * 4,
        out_specs=anywhere,
        scratch_shapes=[
            pltpu.VMEM((6, PADDED, ROWS), jnp.bfloat16),
            pltpu.VMEM(((WINDOW + 8) * PITCH, LANES), jnp.float32),
            pltpu.VMEM((OPS, P_SIZE, P_SIZE), jnp.bfloat16),
            pltpu.VMEM((P_SIZE, OPS * PADDED), jnp.bfloat16),
            pltpu.VMEM((GROUP * TILE * PITCH + 8, LANES), jnp.float32),
            pltpu.VMEM((GROUP * TILE * PITCH + 8, LANES), jnp.float32),
            pltpu.VMEM((SLOTS, ROWS), jnp.int32),
            pltpu.VMEM((SLOTS, ROWS), jnp.int32),
            pltpu.VMEM((LANES, LANES), jnp.int32),
            pltpu.SMEM((LANES, LANES), jnp.int32),
            pltpu.VMEM((P_SIZE, ROWS), jnp.float32),
            pltpu.SemaphoreType.DMA,
            pltpu.SemaphoreType.DMA,
            pltpu.SemaphoreType.DMA,
            pltpu.SemaphoreType.DMA,
            pltpu.SemaphoreType.DMA,
            pltpu.SemaphoreType.DMA((PIECES,)),
            pltpu.SemaphoreType.DMA((5, PIECES)),
            pltpu.SemaphoreType.DMA((5, PIECES)),
        ],
        compiler_params=pltpu.CompilerParams(
            collective_id=0, has_side_effects=True, vmem_limit_bytes=56 * 1024 * 1024
        ),
        name="translate",
    )(multipoles.T, sources.T, labels.T, operators)
    return out.T


def solution(mesh):
    placed = (
        P(("morton", "help"), None),
        P(("morton", "help"), None),
        P(("morton", "help"), None),
        P(),
    )
    return jax.shard_map(
        per_device,
        mesh=mesh,
        in_specs=placed,
        out_specs=P(("morton", "help"), None),
        check_vma=False,
    )
```

time: 48.7 us -> 39.6 us (0.81)
  the two profiles are of different devices: /device:TPU:0 before, /device:TPU:97 now
where the time goes in v2:
time: 39.6 us; the launch traced here: 39.5 us
  Pallas kernels  37 us (93%)
  local copies, waits for them, and re-layouts  2.44 us (6%)
    pallas_call x1, Pallas kernels, per_device(): pl.pallas_call(translate_kernel, out_shape=jax.ShapeDtypeStruct((P_SIZE,...  37 us
    unnamed x1, local copies, waits for them, and re-layouts  2.44 us

profile of v2, /device:TPU:97, one launch (start us, length us, event | category | flops | bytes accessed | tf_op | source)
XLA Modules:
  0.0 39.5 jit_solution(13249382784721400434)
XLA Ops:
  0.0 37.0 %translate.1 = f32[296,1024]{1,0:T(8,128)} custom-call(bf16[296,1024]{1,0:T(8,128)(2,1)} %bitcast.5, s32[16,1024]{1,0:T(8,128)} %bitcast.6, s32[16,1024]{1,0:T(8,128)} %bitcast.7, bf16[16,296,296]{2,1,0:T(8,128)(2,1)} %op_ref.1), custom_call_target="tpu_custom_call" | custom-call | tf_op jit(solution)/shard_map/translate/pallas_call | solution.py:244
  37.0 2.4 %copy.6 = f32[1024,296]{0,1:T(8,128)} copy(f32[1024,296]{0,1:T(8,128)} %bitcast.4) | data formatting | bytes 2424832

commit v3 on v2

--- a/solution.py
+++ b/solution.py
@@ -22,9 +22,9 @@
 
 
 def translate_kernel(
-    mult_ref, src_hbm, lab_hbm, op_ref, out_ref,
-    recv, win, opraw, opt, left_g, right_g, src_ref, lab_ref, idxv, idxs, total,
-    own_sem, src_sem, lab_sem, op_sem, idx_sem, out_sem, send_sem, recv_sem,
+    mult_ref, src_hbm, lab_hbm, op_ref, total,
+    recv, win, opraw, opt, left_g, right_g, src_ref, lab_ref, idxv, idxs,
+    own_sem, src_sem, lab_sem, op_sem, idx_sem, send_sem, recv_sem,
 ):
     g = lax.axis_index("morton")
     h = lax.axis_index("help")
@@ -206,25 +206,23 @@
         else:
             total[:, where] = result
 
-    def leave(n):
-        where = pl.ds(pl.multiple_of(n * TILE, TILE), TILE)
-        return pltpu.make_async_copy(total.at[:, where], out_ref.at[:, where], out_sem.at[n])
-
-    gather(0, 0, left_g)
-
-    @pl.loop(0, blocks)
-    def _(n):
+    def block(n, last):
         for k in range(groups):
             held, into = (right_g, left_g) if k % 2 else (left_g, right_g)
             if k < groups - 1:
                 gather(n, k + 1, into)
-            else:
-                gather(lax.rem(n + 1, blocks), 0, into)
+            elif not last:
+                gather(n + 1, 0, into)
             multiply(n, k, held)
-        leave(n).start()
-
-    for n in range(blocks):
-        leave(n).wait()
+
+    gather(0, 0, left_g)
+
+    @pl.loop(0, blocks - 1)
+    def _(n):
+        block(n, False)
+
+    block(blocks - 1, True)
+
     for b in order:
         sides[b].wait_send()
 
@@ -243,9 +241,9 @@
     anywhere = pl.BlockSpec(memory_space=pl.ANY)
     out = pl.pallas_call(
         translate_kernel,
-        out_shape=jax.ShapeDtypeStruct((P_SIZE, ROWS), jnp.float32),
+        out_shape=pltpu.VMEM((P_SIZE, ROWS), jnp.float32),
         in_specs=[anywhere] * 4,
-        out_specs=anywhere,
+        out_specs=pl.BlockSpec(memory_space=pltpu.VMEM),
         scratch_shapes=[
             pltpu.VMEM((6, PADDED, ROWS), jnp.bfloat16),
             pltpu.VMEM(((WINDOW + 8) * PITCH, LANES), jnp.float32),
@@ -257,18 +255,16 @@
             pltpu.VMEM((SLOTS, ROWS), jnp.int32),
             pltpu.VMEM((LANES, LANES), jnp.int32),
             pltpu.SMEM((LANES, LANES), jnp.int32),
-            pltpu.VMEM((P_SIZE, ROWS), jnp.float32),
-            pltpu.SemaphoreType.DMA,
-            pltpu.SemaphoreType.DMA,
-            pltpu.SemaphoreType.DMA,
-            pltpu.SemaphoreType.DMA,
-            pltpu.SemaphoreType.DMA,
-            pltpu.SemaphoreType.DMA((PIECES,)),
+            pltpu.SemaphoreType.DMA,
+            pltpu.SemaphoreType.DMA,
+            pltpu.SemaphoreType.DMA,
+            pltpu.SemaphoreType.DMA,
+            pltpu.SemaphoreType.DMA,
             pltpu.SemaphoreType.DMA((5, PIECES)),
             pltpu.SemaphoreType.DMA((5, PIECES)),
         ],
         compiler_params=pltpu.CompilerParams(
-            collective_id=0, has_side_effects=True, vmem_limit_bytes=56 * 1024 * 1024
+            collective_id=0, has_side_effects=True, vmem_limit_bytes=58 * 1024 * 1024
         ),
         name="translate",
     )(multipoles.T, sources.T, labels.T, operators)

time: 39.6 us -> 36.8 us (0.929)
  local copies, waits for them, and re-layouts: 2.44 us -> 1.03 us
  Pallas kernels: 37 us -> 35.6 us
    unnamed x1, local copies, waits for them, and re-layouts: 2.44 us -> 1.03 us
    pallas_call x1, Pallas kernels: 37 us -> 35.6 us  [per_device(): pl.pallas_call(translate_kernel, out_shape=pltpu.VMEM((P_SIZE, ROWS), jnp...]
where the time goes in v3:
time: 36.8 us; the launch traced here: 36.7 us
  Pallas kernels  35.6 us (97%)
  local copies, waits for them, and re-layouts  1.03 us (3%)
    pallas_call x1, Pallas kernels, per_device(): pl.pallas_call(translate_kernel, out_shape=pltpu.VMEM((P_SIZE, ROWS), jnp...  35.6 us
    unnamed x1, local copies, waits for them, and re-layouts  1.03 us

profile of v3, /device:TPU:97, one launch (start us, length us, event | category | flops | bytes accessed | tf_op | source)
XLA Modules:
  0.0 36.7 jit_solution(750131317044057272)
XLA Ops:
  0.0 35.6 %translate.1 = f32[296,1024]{1,0:T(8,128)S(1)} custom-call(bf16[296,1024]{1,0:T(8,128)(2,1)} %bitcast.5, s32[16,1024]{1,0:T(8,128)} %bitcast.6, s32[16,1024]{1,0:T(8,128)} %bitcast.7, bf16[16,296,296]{2,1,0:T(8,128)(2,1)} %op_ref.1), custom_call_target="tpu_custom_call" | custom-call | tf_op jit(solution)/shard_map/translate/pallas_call | solution.py:242
  35.6 1.0 %copy.6 = f32[1024,296]{0,1:T(8,128)} copy(f32[1024,296]{0,1:T(8,128)S(1)} %bitcast.4) | data formatting | bytes 2424832

commit v4 on v3

--- a/solution.py
+++ b/solution.py
@@ -13,7 +13,8 @@
 CHUNKS = 3
 PITCH = 4
 PADDED = CHUNKS * LANES
-PIECES = 4
+CUTS = ((0, 256), (256, 256), (512, 256), (768, 128), (896, 128))
+PIECES = len(CUTS)
 WINDOW = 6 * ROWS
 EMPTY = WINDOW
 GROUP = 4
@@ -49,7 +50,7 @@
     pl.semaphore_wait(barrier, 1 + has_above.astype(jnp.int32) + has_below.astype(jnp.int32))
 
     def lanes(b):
-        return pl.ds(b * TILE, TILE)
+        return pl.ds(*CUTS[b])
 
     def send(kind, b, slot, device, source):
         return pltpu.make_async_remote_copy(
@@ -116,12 +117,16 @@
 
     def place(pairs):
         for slot, b in pairs:
+            start, size = CUTS[b]
             turned = lax.dot_general(
-                unit, recv[slot, :, lanes(b)], (((1,), (1,)), ((), ())), preferred_element_type=jnp.float32
+                unit[:size, :size],
+                recv[slot, :, lanes(b)],
+                (((1,), (1,)), ((), ())),
+                preferred_element_type=jnp.float32,
             )
-            base = pl.multiple_of((slot * ROWS + b * TILE) * PITCH, TILE * PITCH)
+            base = pl.multiple_of((slot * ROWS + start) * PITCH, LANES * PITCH)
             for c in range(CHUNKS):
-                win[pl.ds(base + c, TILE, stride=PITCH), :] = turned[:, c * LANES : c * LANES + LANES]
+                win[pl.ds(base + c, size, stride=PITCH), :] = turned[:, c * LANES : c * LANES + LANES]
 
     ops_copy.wait()
     unit_op = eye(P_SIZE)

time: 36.8 us -> 36.5 us (level)
  no operation moved by 1% of the time
where the time goes in v4:
time: 36.5 us; the launch traced here: 36.4 us
  Pallas kernels  35.4 us (97%)
  local copies, waits for them, and re-layouts  1.03 us (3%)
    pallas_call x1, Pallas kernels, per_device(): pl.pallas_call(translate_kernel, out_shape=pltpu.VMEM((P_SIZE, ROWS), jnp...  35.4 us
    unnamed x1, local copies, waits for them, and re-layouts  1.03 us

profile of v4, /device:TPU:97, one launch (start us, length us, event | category | flops | bytes accessed | tf_op | source)
XLA Modules:
  0.0 36.4 jit_solution(6966566503546732181)
XLA Ops:
  0.0 35.4 %translate.1 = f32[296,1024]{1,0:T(8,128)S(1)} custom-call(bf16[296,1024]{1,0:T(8,128)(2,1)} %bitcast.5, s32[16,1024]{1,0:T(8,128)} %bitcast.6, s32[16,1024]{1,0:T(8,128)} %bitcast.7, bf16[16,296,296]{2,1,0:T(8,128)(2,1)} %op_ref.1), custom_call_target="tpu_custom_call" | custom-call | tf_op jit(solution)/shard_map/translate/pallas_call | solution.py:247
  35.4 1.0 %copy.6 = f32[1024,296]{0,1:T(8,128)} copy(f32[1024,296]{0,1:T(8,128)S(1)} %bitcast.4) | data formatting | bytes 2424832
